TPU v7x, 32 devices: a whole 2x2x4 slice. The times are simulated.
32 devices in a mesh: view: 4 (over x, core), bx: 4 (over z), by: 2 (over y).
Axes of the slice: x: 2, y: 2, z: 4, core: 2. Of those that a mesh axis runs over, the one named last changes fastest.
Arguments:
- estimate: float32 [256, 32, 128], P('bx', 'by'), may hold values from 0.5 to 2
- observed: float32 [4, 2048, 512], P('view', ('bx', 'by')), may hold values from 0.25 to 4
- destination: int32 [4, 2048, 1], P('view', ('bx', 'by')), may hold values from 0 to 7; in each aligned block of 256 rows (0 to 255, 256 to 511, ..., all dimensions but the last counted through in order) at most 64 rows name the same one
- slot_index: int32 [4, 2048], P('view', ('bx', 'by')), may hold values from 0 to 255
- valid_count: int32 [4, 2048], P('view', ('bx', 'by')), may hold values from 32 to 128
- blend_weight: float32 [4, 2048], P('view', ('bx', 'by')), may hold values from 0.2 to 1
- kernel_x: float32 [4, 17], P('view'), may hold values from 0.1 to 1
- kernel_y: float32 [4, 17], P('view'), may hold values from 0.1 to 1
- kernel_z: float32 [4, 33], P('view'), may hold values from 0.1 to 1
Outputs:
- updated: float32 [256, 32, 128], P('bx', 'by')
Inputs may be any that keep to these rules, and one draw needn't show every extreme that they name: `destination`: in each view, the 256 rows of one device name no brick more than 64 times, a bound that some block reaches.
All inputs are finite; a program needn't handle non-finite values.
Results may differ from a plain program's by a relative error of at most 0.0001.
Values sent between devices are 32-bit elements; how exact they have to be, the bound alone decides.
No kernel may reach another device: no remote copies, remote signals or barrier semaphores. Data moves between devices by JAX's collectives and lax.ppermute only.
A program may use at most 64 MiB of HBM per device.

v0:
```python
import jax
import jax.numpy as jnp
from jax import lax
from jax.sharding import PartitionSpec as P

R = 8
RZ = 16
YP = 4
PV = 512
SLOTS = 256
PIECES = 256
PRIOR_WEIGHT = 0.5


def with_halo(block, sides, width):
    for axis, dim in sides:
        count = lax.axis_size(axis)
        forward = [(i, i + 1) for i in range(count - 1)]
        backward = [(target, source) for source, target in forward]
        low = lax.ppermute(
            lax.slice_in_dim(block, block.shape[dim] - width, None, axis=dim), axis, forward
        )
        high = lax.ppermute(lax.slice_in_dim(block, 0, width, axis=dim), axis, backward)
        block = jnp.concatenate([low, block, high], axis=dim)
    return block


def band_matrix(kernel, extent, radius):
    spread = jnp.arange(extent + 2 * radius)[None, :] - jnp.arange(extent)[:, None]
    offsets = jnp.arange(2 * radius + 1)
    hits = (spread[:, :, None] == offsets[None, None, :]).astype(jnp.float32)
    return jnp.sum(kernel[None, None, :] * hits, axis=2)


def separable(padded, kernel_a, kernel_b, kernel_c):
    rows_x = padded.shape[0] - 2 * R
    rows_y = padded.shape[1] - 2 * R
    depth_cells = padded.shape[2]
    along_first = jnp.einsum(
        "xe,eyz->xyz", band_matrix(kernel_a, rows_x, R), padded, precision=lax.Precision.HIGHEST
    )
    second = jnp.einsum(
        "ye,xez->xyz",
        band_matrix(kernel_b, rows_y, R),
        along_first,
        precision=lax.Precision.HIGHEST,
    )
    depth_band = band_matrix(kernel_c, depth_cells, RZ)[:, RZ : RZ + depth_cells]
    return jnp.einsum("zw,xyw->xyz", depth_band, second, precision=lax.Precision.HIGHEST)


def local(
    estimate,
    observed,
    destination,
    slot_index,
    valid_count,
    blend_weight,
    kernel_x,
    kernel_y,
    kernel_z,
):
    rows_x, rows_y, depth_cells = estimate.shape
    norm_x = kernel_x[0] / jnp.sum(kernel_x[0])
    norm_y = kernel_y[0] / jnp.sum(kernel_y[0])
    norm_z = kernel_z[0] / jnp.sum(kernel_z[0])
    padded = with_halo(estimate, (("bx", 0), ("by", 1)), R)
    blurred = separable(padded, norm_x, norm_y, norm_z)
    count_bx = lax.axis_size("bx")
    count_by = lax.axis_size("by")
    bricks = count_bx * count_by
    capacity = max(4, 2 * PIECES // bricks)
    target = destination[0, :, 0]
    member = (target[:, None] == jnp.arange(bricks)[None, :]).astype(jnp.int32)
    slot_rank = jnp.sum((jnp.cumsum(member, axis=0) - 1) * member, axis=1)
    send_place = target * capacity + slot_rank
    send_rows = jnp.zeros((bricks * capacity, PV), jnp.float32).at[send_place].set(observed[0])
    send_meta = (
        jnp.zeros((bricks * capacity, 2), jnp.int32)
        .at[send_place]
        .set(jnp.stack([slot_index[0], valid_count[0]], axis=1))
    )
    send_weight = jnp.zeros((bricks * capacity,), jnp.float32).at[send_place].set(blend_weight[0])
    recv_rows, recv_meta, recv_weight = (
        lax.all_to_all(
            send_rows.reshape(bricks, capacity, PV),
            ("bx", "by"),
            split_axis=0,
            concat_axis=0,
            tiled=True,
        ),
        lax.all_to_all(
            send_meta.reshape(bricks, capacity, 2),
            ("bx", "by"),
            split_axis=0,
            concat_axis=0,
            tiled=True,
        ),
        lax.all_to_all(
            send_weight.reshape(bricks, capacity),
            ("bx", "by"),
            split_axis=0,
            concat_axis=0,
            tiled=True,
        ),
    )
    recv_rows = recv_rows.reshape(bricks * capacity, PV)
    recv_meta = recv_meta.reshape(bricks * capacity, 2)
    recv_weight = recv_weight.reshape(bricks * capacity)
    depth_index = jnp.arange(depth_cells, dtype=jnp.int32)
    keep_mask = (depth_index[None, :] < recv_meta[:, 1:2]).astype(jnp.float32) * recv_weight[
        :, None
    ]
    weighted = (recv_rows.reshape(-1, YP, depth_cells) * keep_mask[:, None, :]).reshape(-1, PV)
    chooser = (jnp.arange(SLOTS)[:, None] == recv_meta[:, 0][None, :]).astype(jnp.float32)
    data_slots = jnp.dot(chooser, weighted, precision=lax.Precision.HIGHEST)
    cover_slots = jnp.dot(chooser, keep_mask, precision=lax.Precision.HIGHEST)
    data_volume = data_slots.reshape(rows_x, rows_y, depth_cells)
    cover_wide = jnp.broadcast_to(
        cover_slots.reshape(rows_x, rows_y // YP, 1, depth_cells),
        (rows_x, rows_y // YP, YP, depth_cells),
    )
    cover_volume = cover_wide.reshape(rows_x, rows_y, depth_cells)
    ratio_field = (data_volume + PRIOR_WEIGHT * blurred) / ((cover_volume + PRIOR_WEIGHT) * blurred)
    padded_ratio = with_halo(ratio_field, (("bx", 0), ("by", 1)), R)
    correction = separable(padded_ratio, norm_x[::-1], norm_y[::-1], norm_z[::-1])
    log_term = jnp.log(correction)
    logsum = lax.psum(log_term, "view")
    return estimate * jnp.exp(logsum)


def solution(mesh):
    placed = (
        P("bx", "by", None),
        P("view", ("bx", "by"), None),
        P("view", ("bx", "by"), None),
        P("view", ("bx", "by")),
        P("view", ("bx", "by")),
        P("view", ("bx", "by")),
        P("view", None),
        P("view", None),
        P("view", None),
    )
    return jax.shard_map(
        local, mesh=mesh, in_specs=placed, out_specs=P("bx", "by", None), check_vma=False
    )
```

profile of v0, /device:TPU:0, one launch (start us, length us, event | category | flops | bytes accessed | tf_op | source)
XLA Modules:
  0.0 148.1 jit_solution(831064255658808431)
XLA Ops:
  9.6 1.6 %scatter_custom_fusion.2 = f32[512]{0:T(512)S(1)} fusion(s32[256]{0:T(256)S(1)} %bitcast.81, f32[256]{0:T(256)} %bitcast.89, f32[]{:T(128)} %constant.22.clone.1), kind=kCustom, calls=%fused_computation.64 | custom fusion | bytes 2560 | tf_op jit(solution)/shard_map/scatter | solution.py:83
  11.8 7.3 %all-to-all-start.2 = ((f32[8,1,64]{2,1,0:T(1,128)}), f32[8,1,64]{2,1,0:T(1,128)S(1)}, u32[]{:S(2)}, u32[]{:S(2)}) async-start(f32[8,1,64]{2,1,0:T(1,128)} %all_to_all.14), calls=%async_computation.2 | async-start | bytes 8192 | tf_op jit(solution)/shard_map/all_to_all | solution.py:99
  20.0 3.9 %collective-permute-start = (f32[8,16,128]{2,0,1:T(8,128)S(1)}, f32[8,16,128]{2,0,1:T(8,128)S(1)}, u32[]{:S(2)}, u32[]{:S(2)}) collective-permute-start(f32[8,16,128]{2,0,1:T(8,128)S(1)} %copy.60), channel_id=1, source_target_pairs={{0,2},{2,4},{4,6},{1,3},{3,5},{5,7},{8,10},{10,12},{12,14},{9,11},... | collective-permute-start | bytes 196616 | tf_op jit(solution)/shard_map/ppermute | solution.py:20
  24.0 1.3 collective-permute-start.1
  25.3 1.3 reduce_sum.92
  27.3 1.3 reduce_sum.97
  29.3 1.3 reduce_sum.99
  31.4 1.3 broadcast_divide_fusion.4
  32.7 1.2 broadcast_divide_fusion.2
  33.9 1.3 broadcast_divide_fusion
  38.9 6.6 %all-to-all-start = ((s32[8,1,128]{2,1,0:T(1,128)}), s32[8,1,128]{2,1,0:T(1,128)S(1)}, u32[]{:S(2)}, u32[]{:S(2)}) async-start(s32[8,1,128]{2,1,0:T(1,128)} %reshape.213), calls=%async_computation | async-start | bytes 8192 | tf_op jit(solution)/shard_map/all_to_all | solution.py:92
  45.6 2.5 %scatter_custom_fusion.1 = f32[512,512]{1,0:T(8,128)} fusion(s32[256]{0:T(256)S(1)} %bitcast.83, f32[1,256,512]{2,1,0:T(8,128)S(1)} %copy-done, f32[]{:T(128)} %constant.22.clone.1), kind=kCustom, calls=%fused_computation.28 | custom fusion | bytes 1572868 | tf_op jit(solution)/shard_map/scatter | solution.py:77
  49.5 2.5 %all-to-all-done = s32[8,1,128]{2,1,0:T(1,128)S(1)} async-done(((s32[8,1,128]{2,1,0:T(1,128)}), s32[8,1,128]{2,1,0:T(1,128)S(1)}, u32[]{:S(2)}, u32[]{:S(2)}) %all-to-all-start) | async-done | bytes 4128 | tf_op jit(solution)/shard_map/all_to_all | solution.py:92
  51.9 3.6 %all-to-all-start.1 = ((f32[8,64,512]{2,1,0:T(8,128)}), f32[8,64,512]{2,1,0:T(8,128)S(1)}, u32[]{:S(2)}, u32[]{:S(2)}) async-start(f32[8,64,512]{2,1,0:T(8,128)} %bitcast.14), calls=%async_computation.1 | async-start | bytes 2097152 | tf_op jit(solution)/shard_map/all_to_all | solution.py:85
  57.1 3.9 %collective-permute-start.2 = (f32[80,8,128]{2,0,1:T(8,128)S(1)}, f32[80,8,128]{2,0,1:T(8,128)S(1)}, u32[]{:S(2)}, u32[]{:S(2)}) collective-permute-start(f32[80,8,128]{2,0,1:T(8,128)S(1)} %get-tuple-element.13), channel_id=1, source_target_pairs={{0,1},{2,3},{4,5},{6,7},{8,9},{10,11},{12,13},{14,15},{16,17},{18,... | collective-permute-start | bytes 983048 | tf_op jit(solution)/shard_map/ppermute | solution.py:20
  61.0 1.3 collective-permute-start.3
  63.1 7.8 %collective-permute-done.2 = f32[80,8,128]{2,0,1:T(8,128)S(1)} collective-permute-done((f32[80,8,128]{2,0,1:T(8,128)S(1)}, f32[80,8,128]{2,0,1:T(8,128)S(1)}, u32[]{:S(2)}, u32[]{:S(2)}) %collective-permute-start.2) | collective-permute-done | bytes 327712 | tf_op jit(solution)/shard_map/ppermute | solution.py:20
  70.8 4.3 %collective-permute-done.3 = f32[80,8,128]{2,0,1:T(8,128)S(1)} collective-permute-done((f32[80,8,128]{2,0,1:T(8,128)S(1)}, f32[80,8,128]{2,0,1:T(8,128)S(1)}, u32[]{:S(2)}, u32[]{:S(2)}) %collective-permute-start.3) | collective-permute-done | bytes 327712 | tf_op jit(solution)/shard_map/ppermute | solution.py:23
  76.2 1.3 convolution_bitcast_fusion.1
  77.5 2.3 %all-to-all-done.1 = f32[8,64,512]{2,1,0:T(8,128)S(1)} async-done(((f32[8,64,512]{2,1,0:T(8,128)}), f32[8,64,512]{2,1,0:T(8,128)S(1)}, u32[]{:S(2)}, u32[]{:S(2)}) %all-to-all-start.1) | async-done | bytes 1048608 | tf_op jit(solution)/shard_map/all_to_all | solution.py:85
  81.5 1.7 %collective-permute-start.4 = (f32[8,16,128]{2,1,0:T(8,128)S(1)}, f32[8,16,128]{2,1,0:T(8,128)S(1)}, u32[]{:S(2)}, u32[]{:S(2)}) collective-permute-start(f32[8,16,128]{2,1,0:T(8,128)S(1)} %get-tuple-element.15), channel_id=1, source_target_pairs={{0,2},{2,4},{4,6},{1,3},{3,5},{5,7},{8,10},{10,12},{12,14},{9,11},... | collective-permute-start | bytes 196616 | tf_op jit(solution)/shard_map/ppermute | solution.py:20
  83.2 1.3 collective-permute-start.5
  85.1 4.3 %collective-permute-done.5 = f32[8,16,128]{2,1,0:T(8,128)S(1)} collective-permute-done((f32[8,16,128]{2,1,0:T(8,128)S(1)}, f32[8,16,128]{2,1,0:T(8,128)S(1)}, u32[]{:S(2)}, u32[]{:S(2)}) %collective-permute-start.5) | collective-permute-done | bytes 65568 | tf_op jit(solution)/shard_map/ppermute | solution.py:23
  89.4 2.7 %collective-permute-start.6 = (f32[80,8,128]{2,1,0:T(8,128)S(1)}, f32[80,8,128]{2,1,0:T(8,128)S(1)}, u32[]{:S(2)}, u32[]{:S(2)}) collective-permute-start(f32[80,8,128]{2,1,0:T(8,128)S(1)} %get-tuple-element.11), channel_id=1, source_target_pairs={{0,1},{2,3},{4,5},{6,7},{8,9},{10,11},{12,13},{14,15},{16,17},{18,... | collective-permute-start | bytes 983048 | tf_op jit(solution)/shard_map/ppermute | solution.py:20
  92.2 1.5 collective-permute-start.7
  93.6 3.5 %collective-permute-done.6 = f32[80,8,128]{2,1,0:T(8,128)S(1)} collective-permute-done((f32[80,8,128]{2,1,0:T(8,128)S(1)}, f32[80,8,128]{2,1,0:T(8,128)S(1)}, u32[]{:S(2)}, u32[]{:S(2)}) %collective-permute-start.6) | collective-permute-done | bytes 327712 | tf_op jit(solution)/shard_map/ppermute | solution.py:20
  97.1 4.1 %collective-permute-done.7 = f32[80,8,128]{2,1,0:T(8,128)S(1)} collective-permute-done((f32[80,8,128]{2,1,0:T(8,128)S(1)}, f32[80,8,128]{2,1,0:T(8,128)S(1)}, u32[]{:S(2)}, u32[]{:S(2)}) %collective-permute-start.7) | collective-permute-done | bytes 327712 | tf_op jit(solution)/shard_map/ppermute | solution.py:23
  101.4 1.8 %fusion.6 = f32[64,32,128]{2,0,1:T(8,128)S(1)} fusion(f32[80,32,128]{2,1,0:T(8,128)S(1)} %pad_maximum_fusion, f32[64,80]{1,0:T(8,128)S(1)} %get-tuple-element.7), kind=kOutput, calls=%fused_computation.13 | convolution fusion | flops 251658240 | bytes 2379776 | tf_op jit(solution)/shard_map/xe,eyz->xyz/dot_general | solution.py:39
  103.1 1.3 convolution_bitcast_fusion
  104.4 1.4 convolution_log_fusion
  105.8 33.5 %all-reduce.2.cloned.1.call-done = f32[64,16,128]{2,1,0:T(8,128)} async-done(((f32[64,16,128]{2,1,0:T(8,128)}), f32[64,16,128]{2,1,0:T(8,128)}) %all-reduce.2.cloned.1.call-update) | async-done | bytes 524304 | tf_op jit(solution)/shard_map/psum | solution.py:128
  139.3 1.9 %exponential_multiply_fusion = f32[64,16,128]{2,1,0:T(8,128)} fusion(f32[64,16,128]{2,1,0:T(8,128)S(1)} %copy-done.1, f32[64,16,128]{2,1,0:T(8,128)} %all-reduce.2.cloned.1.call-done), kind=kLoop, calls=%fused_computation.30 | loop fusion | flops 131072 | bytes 1572864 | tf_op jit(solution)/shard_map/mul | solution.py:129
  (60 shorter events, 17.8 us)
Async XLA Ops:
  6.5 39.1 %copy-start = (f32[1,256,512]{2,1,0:T(8,128)S(1)}, f32[1,256,512]{2,1,0:T(8,128)}, u32[]{:S(2)}) copy-start(f32[1,256,512]{2,1,0:T(8,128)} %param.10) | copy-start | bytes 1572868
  11.8 27.1 %all-to-all-start.2 = ((f32[8,1,64]{2,1,0:T(1,128)}), f32[8,1,64]{2,1,0:T(1,128)S(1)}, u32[]{:S(2)}, u32[]{:S(2)}) async-start(f32[8,1,64]{2,1,0:T(1,128)} %all_to_all.14), calls=%async_computation.2 | async-start | bytes 8192 | tf_op jit(solution)/shard_map/all_to_all | solution.py:99
  20.0 36.9 %collective-permute-start = (f32[8,16,128]{2,0,1:T(8,128)S(1)}, f32[8,16,128]{2,0,1:T(8,128)S(1)}, u32[]{:S(2)}, u32[]{:S(2)}) collective-permute-start(f32[8,16,128]{2,0,1:T(8,128)S(1)} %copy.60), channel_id=1, source_target_pairs={{0,2},{2,4},{4,6},{1,3},{3,5},{5,7},{8,10},{10,12},{12,14},{9,11},... | collective-permute-start | bytes 196616 | tf_op jit(solution)/shard_map/ppermute | solution.py:20
  24.0 33.1 %collective-permute-start.1 = (f32[8,16,128]{2,0,1:T(8,128)S(1)}, f32[8,16,128]{2,0,1:T(8,128)S(1)}, u32[]{:S(2)}, u32[]{:S(2)}) collective-permute-start(f32[8,16,128]{2,0,1:T(8,128)S(1)} %copy.61), channel_id=1, source_target_pairs={{2,0},{4,2},{6,4},{3,1},{5,3},{7,5},{10,8},{12,10},{14,12},{11,9},... | collective-permute-start | bytes 196616 | tf_op jit(solution)/shard_map/ppermute | solution.py:23
  38.9 13.0 %all-to-all-start = ((s32[8,1,128]{2,1,0:T(1,128)}), s32[8,1,128]{2,1,0:T(1,128)S(1)}, u32[]{:S(2)}, u32[]{:S(2)}) async-start(s32[8,1,128]{2,1,0:T(1,128)} %reshape.213), calls=%async_computation | async-start | bytes 8192 | tf_op jit(solution)/shard_map/all_to_all | solution.py:92
  48.1 8.8 %copy-start.1 = (f32[64,16,128]{2,1,0:T(8,128)S(1)}, f32[64,16,128]{2,1,0:T(8,128)}, u32[]{:S(2)}) copy-start(f32[64,16,128]{2,1,0:T(8,128)} %param.9) | copy-start | bytes 1572868
  51.9 27.9 %all-to-all-start.1 = ((f32[8,64,512]{2,1,0:T(8,128)}), f32[8,64,512]{2,1,0:T(8,128)S(1)}, u32[]{:S(2)}, u32[]{:S(2)}) async-start(f32[8,64,512]{2,1,0:T(8,128)} %bitcast.14), calls=%async_computation.1 | async-start | bytes 2097152 | tf_op jit(solution)/shard_map/all_to_all | solution.py:85
  55.5 83.9 %all-reduce.2.cloned.1.call-start = ((), (), s32[]{:S(2)}) async-start(), calls=%async_computation.3 | async-start | bytes 1048576 | tf_op jit(solution)/shard_map/psum | solution.py:128
  57.1 13.7 %collective-permute-start.2 = (f32[80,8,128]{2,0,1:T(8,128)S(1)}, f32[80,8,128]{2,0,1:T(8,128)S(1)}, u32[]{:S(2)}, u32[]{:S(2)}) collective-permute-start(f32[80,8,128]{2,0,1:T(8,128)S(1)} %get-tuple-element.13), channel_id=1, source_target_pairs={{0,1},{2,3},{4,5},{6,7},{8,9},{10,11},{12,13},{14,15},{16,17},{18,... | collective-permute-start | bytes 983048 | tf_op jit(solution)/shard_map/ppermute | solution.py:20
  61.0 14.1 %collective-permute-start.3 = (f32[80,8,128]{2,0,1:T(8,128)S(1)}, f32[80,8,128]{2,0,1:T(8,128)S(1)}, u32[]{:S(2)}, u32[]{:S(2)}) collective-permute-start(f32[80,8,128]{2,0,1:T(8,128)S(1)} %get-tuple-element.14), channel_id=1, source_target_pairs={{1,0},{3,2},{5,4},{7,6},{9,8},{11,10},{13,12},{15,14},{17,16},{19,... | collective-permute-start | bytes 983048 | tf_op jit(solution)/shard_map/ppermute | solution.py:23
  81.5 3.6 %collective-permute-start.4 = (f32[8,16,128]{2,1,0:T(8,128)S(1)}, f32[8,16,128]{2,1,0:T(8,128)S(1)}, u32[]{:S(2)}, u32[]{:S(2)}) collective-permute-start(f32[8,16,128]{2,1,0:T(8,128)S(1)} %get-tuple-element.15), channel_id=1, source_target_pairs={{0,2},{2,4},{4,6},{1,3},{3,5},{5,7},{8,10},{10,12},{12,14},{9,11},... | collective-permute-start | bytes 196616 | tf_op jit(solution)/shard_map/ppermute | solution.py:20
  83.2 6.2 %collective-permute-start.5 = (f32[8,16,128]{2,1,0:T(8,128)S(1)}, f32[8,16,128]{2,1,0:T(8,128)S(1)}, u32[]{:S(2)}, u32[]{:S(2)}) collective-permute-start(f32[8,16,128]{2,1,0:T(8,128)S(1)} %get-tuple-element.16), channel_id=1, source_target_pairs={{2,0},{4,2},{6,4},{3,1},{5,3},{7,5},{10,8},{12,10},{14,12},{11,9},... | collective-permute-start | bytes 196616 | tf_op jit(solution)/shard_map/ppermute | solution.py:23
  89.4 7.7 %collective-permute-start.6 = (f32[80,8,128]{2,1,0:T(8,128)S(1)}, f32[80,8,128]{2,1,0:T(8,128)S(1)}, u32[]{:S(2)}, u32[]{:S(2)}) collective-permute-start(f32[80,8,128]{2,1,0:T(8,128)S(1)} %get-tuple-element.11), channel_id=1, source_target_pairs={{0,1},{2,3},{4,5},{6,7},{8,9},{10,11},{12,13},{14,15},{16,17},{18,... | collective-permute-start | bytes 983048 | tf_op jit(solution)/shard_map/ppermute | solution.py:20
  92.2 9.1 %collective-permute-start.7 = (f32[80,8,128]{2,1,0:T(8,128)S(1)}, f32[80,8,128]{2,1,0:T(8,128)S(1)}, u32[]{:S(2)}, u32[]{:S(2)}) collective-permute-start(f32[80,8,128]{2,1,0:T(8,128)S(1)} %get-tuple-element.12), channel_id=1, source_target_pairs={{1,0},{3,2},{5,4},{7,6},{9,8},{11,10},{13,12},{15,14},{17,16},{19,... | collective-permute-start | bytes 983048 | tf_op jit(solution)/shard_map/ppermute | solution.py:23
Sparse Core Ops, SparseCore 0:
  105.9 33.3 all-reduce.1
where the time goes:
time: 149 us; the launch traced here: 148 us
  waiting for transfers between devices  62.8 us (42%)
  starting transfers between devices  35.1 us (24%)
  other arithmetic  15.7 us (11%)
  between operations  13.7 us (9%)
  local copies, waits for them, and re-layouts  12.2 us (8%)
  matrix products  8.59 us (6%)
    psum x1, waiting for transfers between devices, local(): logsum = lax.psum(log_term, 'view')  33.5 us
    ppermute x4, waiting for transfers between devices, with_halo(): lax.ppermute(lax.slice_in_dim(block, 0, width, axis=dim), axis, backward)  12.7 us
    ppermute x4, starting transfers between devices, with_halo(): lax.ppermute(lax.slice_in_dim(block, block.shape[dim] - width, None, axis...  12.2 us
    ppermute x4, waiting for transfers between devices, with_halo(): lax.ppermute(lax.slice_in_dim(block, block.shape[dim] - width, None, axis...  11.8 us
    all_to_all x1, starting transfers between devices, local(): lax.all_to_all(send_weight.reshape(bricks, capacity), ('bx', 'by'), split...  7.31 us
    all_to_all x1, starting transfers between devices, local(): lax.all_to_all(send_meta.reshape(bricks, capacity, 2), ('bx', 'by'), spli...  6.62 us
    ppermute x4, starting transfers between devices, with_halo(): lax.ppermute(lax.slice_in_dim(block, 0, width, axis=dim), axis, backward)  5.35 us
    all_to_all x1, starting transfers between devices, local(): lax.all_to_all(send_rows.reshape(bricks, capacity, PV), ('bx', 'by'), spl...  3.56 us
  transfers between devices with their start and end apart: 12, of which 9 were waited for; matrix products, arithmetic and copies ran while one was open for 16% of the time, Pallas kernels for 0%

commit v1 on v0

--- a/solution.py
+++ b/solution.py
@@ -10,6 +10,22 @@
 SLOTS = 256
 PIECES = 256
 PRIOR_WEIGHT = 0.5
+
+
+def pairwise_exchange(x, axis, split, join):
+    ways, here = (lax.axis_size(axis), lax.axis_index(axis))
+    width = x.shape[split] // ways
+    dims = list(x.shape)
+    dims[split] = width
+    height = dims[join]
+    dims[join] = height * ways
+    full = jnp.zeros(dims, x.dtype)
+    for mask in range(ways):
+        part = lax.dynamic_slice_in_dim(x, (here ^ mask) * width, width, axis=split)
+        if mask:
+            part = lax.ppermute(part, axis, [(d, d ^ mask) for d in range(ways)])
+        full = lax.dynamic_update_slice_in_dim(full, part, (here ^ mask) * height, axis=join)
+    return full
 
 
 def with_halo(block, sides, width):
@@ -89,13 +105,7 @@
             concat_axis=0,
             tiled=True,
         ),
-        lax.all_to_all(
-            send_meta.reshape(bricks, capacity, 2),
-            ("bx", "by"),
-            split_axis=0,
-            concat_axis=0,
-            tiled=True,
-        ),
+        pairwise_exchange(send_meta.reshape(bricks, capacity, 2), ("bx", "by"), 0, 0),
         lax.all_to_all(
             send_weight.reshape(bricks, capacity),
             ("bx", "by"),

time: 149 us -> 143 us (0.960)
  starting transfers between devices: 35.1 us -> 41 us
  other arithmetic: 15.7 us -> 11.1 us
  local copies, waits for them, and re-layouts: 12.2 us -> 8.69 us
  waiting for transfers between devices: 62.8 us -> 59.4 us
    ppermute x0 -> x7, starting transfers between devices: none -> 14.3 us  [pairwise_exchange(): part = lax.ppermute(part, axis, [(d, d ^ mask) for d in range(ways)])]
    ppermute x4, waiting for transfers between devices: 11.8 us -> 3.66 us  [with_halo(): lax.ppermute(lax.slice_in_dim(block, block.shape[dim] - width, None, axis...]
    all_to_all x1 -> x0, starting transfers between devices: 6.62 us -> none  [local(): lax.all_to_all(send_meta.reshape(bricks, capacity, 2), ('bx', 'by'), spli...]
    ppermute x4, waiting for transfers between devices: 12.7 us -> 18.9 us  [with_halo(): lax.ppermute(lax.slice_in_dim(block, 0, width, axis=dim), axis, backward)]
    all_to_all x1 -> x0, waiting for transfers between devices: 2.46 us -> none  [local(): lax.all_to_all(send_meta.reshape(bricks, capacity, 2), ('bx', 'by'), spli...]
    all_to_all x1, starting transfers between devices: 7.31 us -> 4.88 us  [local(): lax.all_to_all(send_weight.reshape(bricks, capacity), ('bx', 'by'), split...]
    all_to_all x1, starting transfers between devices: 3.56 us -> 5.8 us  [local(): lax.all_to_all(send_rows.reshape(bricks, capacity, PV), ('bx', 'by'), spl...]
    another operation x4, local copies, waits for them, and re-layouts: 2.24 us -> 0.29 us
  transfers between devices with their start and end apart: 12 -> 18, of which waited for: 9 -> 8; matrix products, arithmetic and copies ran while one was open for 16% -> 10% of each run, Pallas kernels for 0% -> 0%
where the time goes in v1:
time: 143 us
  waiting for transfers between devices  59.4 us (42%)
  starting transfers between devices  41 us (29%)
  between operations  13.9 us (10%)
  other arithmetic  11.1 us (8%)
  local copies, waits for them, and re-layouts  8.69 us (6%)
  matrix products  8.59 us (6%)
    psum x1, waiting for transfers between devices, local(): logsum = lax.psum(log_term, 'view')  32.9 us
    ppermute x4, waiting for transfers between devices, with_halo(): lax.ppermute(lax.slice_in_dim(block, 0, width, axis=dim), axis, backward)  18.9 us
    ppermute x7, starting transfers between devices, pairwise_exchange(): part = lax.ppermute(part, axis, [(d, d ^ mask) for d in range(ways)])  14.3 us
    ppermute x4, starting transfers between devices, with_halo(): lax.ppermute(lax.slice_in_dim(block, block.shape[dim] - width, None, axis...  10.6 us
    all_to_all x1, starting transfers between devices, local(): lax.all_to_all(send_rows.reshape(bricks, capacity, PV), ('bx', 'by'), spl...  5.8 us
    ppermute x4, starting transfers between devices, with_halo(): lax.ppermute(lax.slice_in_dim(block, 0, width, axis=dim), axis, backward)  5.35 us
    all_to_all x1, starting transfers between devices, local(): lax.all_to_all(send_weight.reshape(bricks, capacity), ('bx', 'by'), split...  4.88 us
    ppermute x4, waiting for transfers between devices, with_halo(): lax.ppermute(lax.slice_in_dim(block, block.shape[dim] - width, None, axis...  3.66 us
  transfers between devices with their start and end apart: 18, of which 8 were waited for; matrix products, arithmetic and copies ran while one was open for 10% of the time, Pallas kernels for 0%

profile of v1, /device:TPU:0, one launch (start us, length us, event | category | flops | bytes accessed | tf_op | source)
XLA Modules:
  0.0 142.7 jit_solution(4774548977951901644)
XLA Ops:
  10.5 1.2 scatter_custom_fusion
  11.8 3.1 %collective-permute-start = (s32[1,64,2]{2,1,0:T(8,128)S(1)}, s32[1,64,2]{2,1,0:T(8,128)S(1)}, u32[]{:S(2)}, u32[]{:S(2)}) collective-permute-start(s32[1,64,2]{2,1,0:T(8,128)S(1)} %get-tuple-element.25), channel_id=1, source_target_pairs={{0,1},{1,0},{2,3},{3,2},{4,5},{5,4},{6,7},{7,6},{8,9},{9,8},{10,11... | collective-permute-start | bytes 1544 | tf_op jit(solution)/shard_map/ppermute | solution.py:26
  14.8 1.6 %collective-permute-start.1 = (s32[1,64,2]{2,1,0:T(8,128)S(1)}, s32[1,64,2]{2,1,0:T(8,128)S(1)}, u32[]{:S(2)}, u32[]{:S(2)}) collective-permute-start(s32[1,64,2]{2,1,0:T(8,128)S(1)} %get-tuple-element.24), channel_id=1, source_target_pairs={{0,2},{1,3},{2,0},{3,1},{4,6},{5,7},{6,4},{7,5},{8,10},{9,11},{10,... | collective-permute-start | bytes 1544 | tf_op jit(solution)/shard_map/ppermute | solution.py:26
  16.4 3.0 %collective-permute-start.3 = (s32[1,64,2]{2,1,0:T(8,128)S(1)}, s32[1,64,2]{2,1,0:T(8,128)S(1)}, u32[]{:S(2)}, u32[]{:S(2)}) collective-permute-start(s32[1,64,2]{2,1,0:T(8,128)S(1)} %get-tuple-element.22), channel_id=1, source_target_pairs={{0,4},{1,5},{2,6},{3,7},{4,0},{5,1},{6,2},{7,3},{8,12},{9,13},{10,... | collective-permute-start | bytes 1544 | tf_op jit(solution)/shard_map/ppermute | solution.py:26
  19.4 1.3 collective-permute-start.4
  20.7 1.6 %scatter_custom_fusion.2 = f32[512]{0:T(512)S(1)} fusion(s32[256]{0:T(256)S(1)} %bitcast.78, f32[256]{0:T(256)} %bitcast.85, f32[]{:T(128)} %constant.16.clone.1), kind=kCustom, calls=%fused_computation.72 | custom fusion | bytes 2560 | tf_op jit(solution)/shard_map/scatter | solution.py:99
  22.9 4.9 %all-to-all-start.1 = ((f32[8,1,64]{2,1,0:T(1,128)}), f32[8,1,64]{2,1,0:T(1,128)S(1)}, u32[]{:S(2)}, u32[]{:S(2)}) async-start(f32[8,1,64]{2,1,0:T(1,128)} %all_to_all.10), calls=%async_computation.1 | async-start | bytes 8192 | tf_op jit(solution)/shard_map/all_to_all | solution.py:109
  32.9 2.5 %scatter_custom_fusion.1 = f32[512,512]{1,0:T(8,128)} fusion(s32[256]{0:T(256)S(1)} %bitcast.79, f32[1,256,512]{2,1,0:T(8,128)S(1)} %copy-done, f32[]{:T(128)} %constant.16.clone.1), kind=kCustom, calls=%fused_computation.28 | custom fusion | bytes 1572868 | tf_op jit(solution)/shard_map/scatter | solution.py:93
  35.5 3.9 %collective-permute-start.5 = (s32[1,64,2]{2,1,0:T(8,128)S(1)}, s32[1,64,2]{2,1,0:T(8,128)S(1)}, u32[]{:S(2)}, u32[]{:S(2)}) collective-permute-start(s32[1,64,2]{2,1,0:T(8,128)S(1)} %get-tuple-element.20), channel_id=1, source_target_pairs={{0,6},{1,7},{2,4},{3,5},{4,2},{5,3},{6,0},{7,1},{8,14},{9,15},{10,... | collective-permute-start | bytes 1544 | tf_op jit(solution)/shard_map/ppermute | solution.py:26
  39.5 1.5 %collective-permute-start.6 = (s32[1,64,2]{2,1,0:T(8,128)S(1)}, s32[1,64,2]{2,1,0:T(8,128)S(1)}, u32[]{:S(2)}, u32[]{:S(2)}) collective-permute-start(s32[1,64,2]{2,1,0:T(8,128)S(1)} %get-tuple-element.19), channel_id=1, source_target_pairs={{0,7},{1,6},{2,5},{3,4},{4,3},{5,2},{6,1},{7,0},{8,15},{9,14},{10,... | collective-permute-start | bytes 1544 | tf_op jit(solution)/shard_map/ppermute | solution.py:26
  41.2 1.6 %collective-permute-start.7 = (f32[8,16,128]{2,0,1:T(8,128)S(1)}, f32[8,16,128]{2,0,1:T(8,128)S(1)}, u32[]{:S(2)}, u32[]{:S(2)}) collective-permute-start(f32[8,16,128]{2,0,1:T(8,128)S(1)} %copy.56), channel_id=1, source_target_pairs={{0,2},{2,4},{4,6},{1,3},{3,5},{5,7},{8,10},{10,12},{12,14},{9,11},... | collective-permute-start | bytes 196616 | tf_op jit(solution)/shard_map/ppermute | solution.py:36
  42.8 1.3 collective-permute-start.8
  44.5 1.7 %collective-permute-done.6 = s32[1,64,2]{2,1,0:T(8,128)S(1)} collective-permute-done((s32[1,64,2]{2,1,0:T(8,128)S(1)}, s32[1,64,2]{2,1,0:T(8,128)S(1)}, u32[]{:S(2)}, u32[]{:S(2)}) %collective-permute-start.6) | collective-permute-done | bytes 544 | tf_op jit(solution)/shard_map/ppermute | solution.py:26
  46.4 5.8 %all-to-all-start = ((f32[8,64,512]{2,1,0:T(8,128)}), f32[8,64,512]{2,1,0:T(8,128)S(1)}, u32[]{:S(2)}, u32[]{:S(2)}) async-start(f32[8,64,512]{2,1,0:T(8,128)} %bitcast.14), calls=%async_computation | async-start | bytes 2097152 | tf_op jit(solution)/shard_map/all_to_all | solution.py:101
  53.8 1.3 collective-permute-start.10
  55.1 4.6 %collective-permute-start.9 = (f32[80,8,128]{2,0,1:T(8,128)S(1)}, f32[80,8,128]{2,0,1:T(8,128)S(1)}, u32[]{:S(2)}, u32[]{:S(2)}) collective-permute-start(f32[80,8,128]{2,0,1:T(8,128)S(1)} %get-tuple-element.13), channel_id=1, source_target_pairs={{0,1},{2,3},{4,5},{6,7},{8,9},{10,11},{12,13},{14,15},{16,17},{18,... | collective-permute-start | bytes 983048 | tf_op jit(solution)/shard_map/ppermute | solution.py:36
  60.4 10.2 %collective-permute-done.10 = f32[80,8,128]{2,0,1:T(8,128)S(1)} collective-permute-done((f32[80,8,128]{2,0,1:T(8,128)S(1)}, f32[80,8,128]{2,0,1:T(8,128)S(1)}, u32[]{:S(2)}, u32[]{:S(2)}) %collective-permute-start.10) | collective-permute-done | bytes 327712 | tf_op jit(solution)/shard_map/ppermute | solution.py:39
  70.6 1.0 fusion
  71.6 1.3 convolution_bitcast_fusion.1
  72.9 2.2 %all-to-all-done = f32[8,64,512]{2,1,0:T(8,128)S(1)} async-done(((f32[8,64,512]{2,1,0:T(8,128)}), f32[8,64,512]{2,1,0:T(8,128)S(1)}, u32[]{:S(2)}, u32[]{:S(2)}) %all-to-all-start) | async-done | bytes 1048608 | tf_op jit(solution)/shard_map/all_to_all | solution.py:101
  76.8 1.7 %collective-permute-start.11 = (f32[8,16,128]{2,1,0:T(8,128)S(1)}, f32[8,16,128]{2,1,0:T(8,128)S(1)}, u32[]{:S(2)}, u32[]{:S(2)}) collective-permute-start(f32[8,16,128]{2,1,0:T(8,128)S(1)} %get-tuple-element.15), channel_id=1, source_target_pairs={{0,2},{2,4},{4,6},{1,3},{3,5},{5,7},{8,10},{10,12},{12,14},{9,11},... | collective-permute-start | bytes 196616 | tf_op jit(solution)/shard_map/ppermute | solution.py:36
  78.5 1.3 collective-permute-start.12
  80.4 4.3 %collective-permute-done.12 = f32[8,16,128]{2,1,0:T(8,128)S(1)} collective-permute-done((f32[8,16,128]{2,1,0:T(8,128)S(1)}, f32[8,16,128]{2,1,0:T(8,128)S(1)}, u32[]{:S(2)}, u32[]{:S(2)}) %collective-permute-start.12) | collective-permute-done | bytes 65568 | tf_op jit(solution)/shard_map/ppermute | solution.py:39
  84.8 2.7 %collective-permute-start.13 = (f32[80,8,128]{2,1,0:T(8,128)S(1)}, f32[80,8,128]{2,1,0:T(8,128)S(1)}, u32[]{:S(2)}, u32[]{:S(2)}) collective-permute-start(f32[80,8,128]{2,1,0:T(8,128)S(1)} %get-tuple-element.11), channel_id=1, source_target_pairs={{0,1},{2,3},{4,5},{6,7},{8,9},{10,11},{12,13},{14,15},{16,17},{18,... | collective-permute-start | bytes 983048 | tf_op jit(solution)/shard_map/ppermute | solution.py:36
  87.5 1.5 %collective-permute-start.14 = (f32[80,8,128]{2,1,0:T(8,128)S(1)}, f32[80,8,128]{2,1,0:T(8,128)S(1)}, u32[]{:S(2)}, u32[]{:S(2)}) collective-permute-start(f32[80,8,128]{2,1,0:T(8,128)S(1)} %get-tuple-element.12), channel_id=1, source_target_pairs={{1,0},{3,2},{5,4},{7,6},{9,8},{11,10},{13,12},{15,14},{17,16},{19,... | collective-permute-start | bytes 983048 | tf_op jit(solution)/shard_map/ppermute | solution.py:39
  89.0 3.1 %collective-permute-done.13 = f32[80,8,128]{2,1,0:T(8,128)S(1)} collective-permute-done((f32[80,8,128]{2,1,0:T(8,128)S(1)}, f32[80,8,128]{2,1,0:T(8,128)S(1)}, u32[]{:S(2)}, u32[]{:S(2)}) %collective-permute-start.13) | collective-permute-done | bytes 327712 | tf_op jit(solution)/shard_map/ppermute | solution.py:36
  92.0 4.4 %collective-permute-done.14 = f32[80,8,128]{2,1,0:T(8,128)S(1)} collective-permute-done((f32[80,8,128]{2,1,0:T(8,128)S(1)}, f32[80,8,128]{2,1,0:T(8,128)S(1)}, u32[]{:S(2)}, u32[]{:S(2)}) %collective-permute-start.14) | collective-permute-done | bytes 327712 | tf_op jit(solution)/shard_map/ppermute | solution.py:39
  96.6 1.8 %fusion.6 = f32[64,32,128]{2,0,1:T(8,128)S(1)} fusion(f32[80,32,128]{2,1,0:T(8,128)S(1)} %pad_maximum_fusion, f32[64,80]{1,0:T(8,128)S(1)} %get-tuple-element.7), kind=kOutput, calls=%fused_computation.13 | convolution fusion | flops 251658240 | bytes 2379776 | tf_op jit(solution)/shard_map/xe,eyz->xyz/dot_general | solution.py:55
  98.3 1.3 convolution_bitcast_fusion
  99.6 1.4 convolution_log_fusion
  101.0 32.9 %all-reduce.2.cloned.1.call-done = f32[64,16,128]{2,1,0:T(8,128)} async-done(((f32[64,16,128]{2,1,0:T(8,128)}), f32[64,16,128]{2,1,0:T(8,128)}) %all-reduce.2.cloned.1.call-update) | async-done | bytes 524304 | tf_op jit(solution)/shard_map/psum | solution.py:138
  133.9 1.9 %exponential_multiply_fusion = f32[64,16,128]{2,1,0:T(8,128)} fusion(f32[64,16,128]{2,1,0:T(8,128)S(1)} %copy-done.1, f32[64,16,128]{2,1,0:T(8,128)} %all-reduce.2.cloned.1.call-done), kind=kLoop, calls=%fused_computation.30 | loop fusion | flops 131072 | bytes 1572864 | tf_op jit(solution)/shard_map/mul | solution.py:139
  (90 shorter events, 15.2 us)
Async XLA Ops:
  6.5 26.4 %copy-start = (f32[1,256,512]{2,1,0:T(8,128)S(1)}, f32[1,256,512]{2,1,0:T(8,128)}, u32[]{:S(2)}) copy-start(f32[1,256,512]{2,1,0:T(8,128)} %param.10) | copy-start | bytes 1572868
  6.5 21.3 %copy-start.1 = (f32[64,16,128]{2,1,0:T(8,128)S(1)}, f32[64,16,128]{2,1,0:T(8,128)}, u32[]{:S(2)}) copy-start(f32[64,16,128]{2,1,0:T(8,128)} %param.9) | copy-start | bytes 1572868
  6.5 21.3 %copy-start.2 = (f32[1,17]{1,0:T(1,128)S(1)}, f32[1,17]{1,0:T(1,128)}, u32[]{:S(2)}) copy-start(f32[1,17]{1,0:T(1,128)} %param.15) | copy-start | bytes 208
  6.5 22.1 %copy-start.3 = (f32[1,17]{1,0:T(1,128)S(1)}, f32[1,17]{1,0:T(1,128)}, u32[]{:S(2)}) copy-start(f32[1,17]{1,0:T(1,128)} %param.16) | copy-start | bytes 208
  6.5 22.8 %copy-start.4 = (f32[1,33]{1,0:T(1,128)S(1)}, f32[1,33]{1,0:T(1,128)}, u32[]{:S(2)}) copy-start(f32[1,33]{1,0:T(1,128)} %param.17) | copy-start | bytes 400
  11.8 23.7 %collective-permute-start = (s32[1,64,2]{2,1,0:T(8,128)S(1)}, s32[1,64,2]{2,1,0:T(8,128)S(1)}, u32[]{:S(2)}, u32[]{:S(2)}) collective-permute-start(s32[1,64,2]{2,1,0:T(8,128)S(1)} %get-tuple-element.25), channel_id=1, source_target_pairs={{0,1},{1,0},{2,3},{3,2},{4,5},{5,4},{6,7},{7,6},{8,9},{9,8},{10,11... | collective-permute-start | bytes 1544 | tf_op jit(solution)/shard_map/ppermute | solution.py:26
  14.8 24.7 %collective-permute-start.1 = (s32[1,64,2]{2,1,0:T(8,128)S(1)}, s32[1,64,2]{2,1,0:T(8,128)S(1)}, u32[]{:S(2)}, u32[]{:S(2)}) collective-permute-start(s32[1,64,2]{2,1,0:T(8,128)S(1)} %get-tuple-element.24), channel_id=1, source_target_pairs={{0,2},{1,3},{2,0},{3,1},{4,6},{5,7},{6,4},{7,5},{8,10},{9,11},{10,... | collective-permute-start | bytes 1544 | tf_op jit(solution)/shard_map/ppermute | solution.py:26
  16.4 24.7 %collective-permute-start.2 = (s32[1,64,2]{2,1,0:T(8,128)S(1)}, s32[1,64,2]{2,1,0:T(8,128)S(1)}, u32[]{:S(2)}, u32[]{:S(2)}) collective-permute-start(s32[1,64,2]{2,1,0:T(8,128)S(1)} %get-tuple-element.23), channel_id=1, source_target_pairs={{0,3},{1,2},{2,1},{3,0},{4,7},{5,6},{6,5},{7,4},{8,11},{9,10},{10,... | collective-permute-start | bytes 1544 | tf_op jit(solution)/shard_map/ppermute | solution.py:26
  16.4 26.4 %collective-permute-start.3 = (s32[1,64,2]{2,1,0:T(8,128)S(1)}, s32[1,64,2]{2,1,0:T(8,128)S(1)}, u32[]{:S(2)}, u32[]{:S(2)}) collective-permute-start(s32[1,64,2]{2,1,0:T(8,128)S(1)} %get-tuple-element.22), channel_id=1, source_target_pairs={{0,4},{1,5},{2,6},{3,7},{4,0},{5,1},{6,2},{7,3},{8,12},{9,13},{10,... | collective-permute-start | bytes 1544 | tf_op jit(solution)/shard_map/ppermute | solution.py:26
  19.4 24.8 %collective-permute-start.4 = (s32[1,64,2]{2,1,0:T(8,128)S(1)}, s32[1,64,2]{2,1,0:T(8,128)S(1)}, u32[]{:S(2)}, u32[]{:S(2)}) collective-permute-start(s32[1,64,2]{2,1,0:T(8,128)S(1)} %get-tuple-element.21), channel_id=1, source_target_pairs={{0,5},{1,4},{2,7},{3,6},{4,1},{5,0},{6,3},{7,2},{8,13},{9,12},{10,... | collective-permute-start | bytes 1544 | tf_op jit(solution)/shard_map/ppermute | solution.py:26
  22.9 23.5 %all-to-all-start.1 = ((f32[8,1,64]{2,1,0:T(1,128)}), f32[8,1,64]{2,1,0:T(1,128)S(1)}, u32[]{:S(2)}, u32[]{:S(2)}) async-start(f32[8,1,64]{2,1,0:T(1,128)} %all_to_all.10), calls=%async_computation.1 | async-start | bytes 8192 | tf_op jit(solution)/shard_map/all_to_all | solution.py:109
  35.5 8.8 %collective-permute-start.5 = (s32[1,64,2]{2,1,0:T(8,128)S(1)}, s32[1,64,2]{2,1,0:T(8,128)S(1)}, u32[]{:S(2)}, u32[]{:S(2)}) collective-permute-start(s32[1,64,2]{2,1,0:T(8,128)S(1)} %get-tuple-element.20), channel_id=1, source_target_pairs={{0,6},{1,7},{2,4},{3,5},{4,2},{5,3},{6,0},{7,1},{8,14},{9,15},{10,... | collective-permute-start | bytes 1544 | tf_op jit(solution)/shard_map/ppermute | solution.py:26
  39.5 6.7 %collective-permute-start.6 = (s32[1,64,2]{2,1,0:T(8,128)S(1)}, s32[1,64,2]{2,1,0:T(8,128)S(1)}, u32[]{:S(2)}, u32[]{:S(2)}) collective-permute-start(s32[1,64,2]{2,1,0:T(8,128)S(1)} %get-tuple-element.19), channel_id=1, source_target_pairs={{0,7},{1,6},{2,5},{3,4},{4,3},{5,2},{6,1},{7,0},{8,15},{9,14},{10,... | collective-permute-start | bytes 1544 | tf_op jit(solution)/shard_map/ppermute | solution.py:26
  41.2 12.3 %collective-permute-start.7 = (f32[8,16,128]{2,0,1:T(8,128)S(1)}, f32[8,16,128]{2,0,1:T(8,128)S(1)}, u32[]{:S(2)}, u32[]{:S(2)}) collective-permute-start(f32[8,16,128]{2,0,1:T(8,128)S(1)} %copy.56), channel_id=1, source_target_pairs={{0,2},{2,4},{4,6},{1,3},{3,5},{5,7},{8,10},{10,12},{12,14},{9,11},... | collective-permute-start | bytes 196616 | tf_op jit(solution)/shard_map/ppermute | solution.py:36
  42.8 10.8 %collective-permute-start.8 = (f32[8,16,128]{2,0,1:T(8,128)S(1)}, f32[8,16,128]{2,0,1:T(8,128)S(1)}, u32[]{:S(2)}, u32[]{:S(2)}) collective-permute-start(f32[8,16,128]{2,0,1:T(8,128)S(1)} %copy.57), channel_id=1, source_target_pairs={{2,0},{4,2},{6,4},{3,1},{5,3},{7,5},{10,8},{12,10},{14,12},{11,9},... | collective-permute-start | bytes 196616 | tf_op jit(solution)/shard_map/ppermute | solution.py:39
  46.4 28.7 %all-to-all-start = ((f32[8,64,512]{2,1,0:T(8,128)}), f32[8,64,512]{2,1,0:T(8,128)S(1)}, u32[]{:S(2)}, u32[]{:S(2)}) async-start(f32[8,64,512]{2,1,0:T(8,128)} %bitcast.14), calls=%async_computation | async-start | bytes 2097152 | tf_op jit(solution)/shard_map/all_to_all | solution.py:101
  52.2 81.7 %all-reduce.2.cloned.1.call-start = ((), (), s32[]{:S(2)}) async-start(), calls=%async_computation.2 | async-start | bytes 1048576 | tf_op jit(solution)/shard_map/psum | solution.py:138
  53.8 16.8 %collective-permute-start.10 = (f32[80,8,128]{2,0,1:T(8,128)S(1)}, f32[80,8,128]{2,0,1:T(8,128)S(1)}, u32[]{:S(2)}, u32[]{:S(2)}) collective-permute-start(f32[80,8,128]{2,0,1:T(8,128)S(1)} %get-tuple-element.14), channel_id=1, source_target_pairs={{1,0},{3,2},{5,4},{7,6},{9,8},{11,10},{13,12},{15,14},{17,16},{19,... | collective-permute-start | bytes 983048 | tf_op jit(solution)/shard_map/ppermute | solution.py:39
  55.1 15.5 %collective-permute-start.9 = (f32[80,8,128]{2,0,1:T(8,128)S(1)}, f32[80,8,128]{2,0,1:T(8,128)S(1)}, u32[]{:S(2)}, u32[]{:S(2)}) collective-permute-start(f32[80,8,128]{2,0,1:T(8,128)S(1)} %get-tuple-element.13), channel_id=1, source_target_pairs={{0,1},{2,3},{4,5},{6,7},{8,9},{10,11},{12,13},{14,15},{16,17},{18,... | collective-permute-start | bytes 983048 | tf_op jit(solution)/shard_map/ppermute | solution.py:36
  76.8 3.6 %collective-permute-start.11 = (f32[8,16,128]{2,1,0:T(8,128)S(1)}, f32[8,16,128]{2,1,0:T(8,128)S(1)}, u32[]{:S(2)}, u32[]{:S(2)}) collective-permute-start(f32[8,16,128]{2,1,0:T(8,128)S(1)} %get-tuple-element.15), channel_id=1, source_target_pairs={{0,2},{2,4},{4,6},{1,3},{3,5},{5,7},{8,10},{10,12},{12,14},{9,11},... | collective-permute-start | bytes 196616 | tf_op jit(solution)/shard_map/ppermute | solution.py:36
  78.5 6.2 %collective-permute-start.12 = (f32[8,16,128]{2,1,0:T(8,128)S(1)}, f32[8,16,128]{2,1,0:T(8,128)S(1)}, u32[]{:S(2)}, u32[]{:S(2)}) collective-permute-start(f32[8,16,128]{2,1,0:T(8,128)S(1)} %get-tuple-element.16), channel_id=1, source_target_pairs={{2,0},{4,2},{6,4},{3,1},{5,3},{7,5},{10,8},{12,10},{14,12},{11,9},... | collective-permute-start | bytes 196616 | tf_op jit(solution)/shard_map/ppermute | solution.py:39
  84.8 7.3 %collective-permute-start.13 = (f32[80,8,128]{2,1,0:T(8,128)S(1)}, f32[80,8,128]{2,1,0:T(8,128)S(1)}, u32[]{:S(2)}, u32[]{:S(2)}) collective-permute-start(f32[80,8,128]{2,1,0:T(8,128)S(1)} %get-tuple-element.11), channel_id=1, source_target_pairs={{0,1},{2,3},{4,5},{6,7},{8,9},{10,11},{12,13},{14,15},{16,17},{18,... | collective-permute-start | bytes 983048 | tf_op jit(solution)/shard_map/ppermute | solution.py:36
  87.5 9.0 %collective-permute-start.14 = (f32[80,8,128]{2,1,0:T(8,128)S(1)}, f32[80,8,128]{2,1,0:T(8,128)S(1)}, u32[]{:S(2)}, u32[]{:S(2)}) collective-permute-start(f32[80,8,128]{2,1,0:T(8,128)S(1)} %get-tuple-element.12), channel_id=1, source_target_pairs={{1,0},{3,2},{5,4},{7,6},{9,8},{11,10},{13,12},{15,14},{17,16},{19,... | collective-permute-start | bytes 983048 | tf_op jit(solution)/shard_map/ppermute | solution.py:39
Sparse Core Ops, SparseCore 0:
  101.1 32.7 all-reduce.1
